TPU v7x, 512 devices: a whole 4x8x8 slice. The times are simulated.
512 devices in a mesh: req: 64 (over z, x, core), tp: 8 (over y).
Axes of the slice: x: 4, y: 8, z: 8, core: 2. Of those that a mesh axis runs over, the one named last changes fastest.
Arguments:
- queries: bfloat16 [1024, 2560], P('req', 'tp'), may hold values from -64 to 64
- fresh_kv: bfloat16 [1024, 1280], P('req', 'tp'), may hold values from -9 to 9
- kv_cache: bfloat16 [8, 160, 655360], P('tp', None, 'req'), may hold values from -6 to 6
- out_weight: bfloat16 [2560, 2560], P('tp'), may hold values from -1.1953125 to 1.1953125
- offsets: int32 [1024], replicated, may hold values from 0 to 655358, as said below
- lengths: int32 [1024], replicated, may hold values from 2 to 8192, as said below
Outputs:
- mixed_out: bfloat16 [1024, 2560], P('req', 'tp')
Inputs may be any that keep to these rules, and one draw needn't show every extreme that they name: Request r belongs to index floor(r / 16) of req and its cache to index floor(offsets[r] / 10240), where it lies whole: offsets[r] + lengths[r] <= (floor(offsets[r] / 10240) + 1) * 10240; caches never intersect. The first 8 requests of each index have their caches on that index; every index holds the caches of exactly 8 requests of other indices, and those of one index's other requests lie on distinct indices. `lengths`: on every index of req one held cache has exactly 8192 tokens.
All inputs are finite; a program needn't handle non-finite values.
Results may differ from a plain program's by a relative error of at most 0.019.
Values may be sent and summed in bfloat16 or wider, within the bound.
No kernel may reach another device: no remote copies, remote signals or barrier semaphores. Data moves between devices by JAX's collectives and lax.ppermute only.
A program may use at most 64 MiB of HBM per device.

v0:
```python
import jax
import jax.numpy as jnp
from jax import lax
from jax.sharding import PartitionSpec as P

HD = 80
W = 4096


def attend(queries, fresh_kv, cache_block, starts, lengths):
    row_count = queries.shape[0]
    kv_heads = cache_block.shape[0]
    tokens = cache_block.shape[2]
    score_scale = HD ** (-0.5)
    grouped = queries.reshape(row_count, kv_heads, -1, HD)
    fresh_split = fresh_kv.reshape(row_count, kv_heads, 2, HD)
    scores = (
        jnp.einsum(
            "nhgd,hdt->hngt", grouped, cache_block[:, :HD, :], preferred_element_type=jnp.float32
        )
        * score_scale
    )
    positions = jnp.arange(tokens, dtype=jnp.int32)[None, :]
    window_end = (starts + lengths)[:, None]
    inside = (
        (positions >= starts[:, None])
        & (positions < window_end)
        & (positions >= window_end - (W - 1))
    )
    scores = jnp.where(inside[None, :, None, :], scores, -jnp.inf)
    own_score = (
        jnp.einsum(
            "nhgd,nhd->hng", grouped, fresh_split[:, :, 0, :], preferred_element_type=jnp.float32
        )
        * score_scale
    )
    highest = jnp.maximum(jnp.max(scores, axis=3), own_score)
    weights = jnp.exp(scores - highest[..., None])
    own_weight = jnp.exp(own_score - highest)
    totals = jnp.sum(weights, axis=3) + own_weight
    summed = jnp.einsum(
        "hngt,hdt->nhgd",
        weights.astype(jnp.bfloat16),
        cache_block[:, HD:, :],
        preferred_element_type=jnp.float32,
    )
    summed = summed + jnp.einsum(
        "hng,nhd->nhgd",
        own_weight.astype(jnp.bfloat16),
        fresh_split[:, :, 1, :],
        preferred_element_type=jnp.float32,
    )
    normed = summed / jnp.transpose(totals, (1, 0, 2))[..., None]
    return normed.astype(jnp.bfloat16).reshape(row_count, -1)


def shards(queries, fresh_kv, kv_cache, out_weight, offsets, lengths):
    devices = lax.axis_size("req")
    device_index = lax.axis_index("req")
    row_count = queries.shape[0]
    half_rows = row_count // 2
    shard_tokens = kv_cache.shape[2]
    shard_start = device_index * shard_tokens
    owner_table = (offsets // shard_tokens).reshape(devices, row_count)
    far_owners = owner_table[:, half_rows:]
    my_owners = lax.dynamic_slice_in_dim(far_owners, device_index, 1, 0)[0]
    home_first = device_index * row_count
    local_out = attend(
        queries[:half_rows],
        fresh_kv[:half_rows],
        kv_cache,
        lax.dynamic_slice_in_dim(offsets, home_first, half_rows) - shard_start,
        lax.dynamic_slice_in_dim(lengths, home_first, half_rows),
    )
    sent_queries, sent_fresh = (
        lax.all_gather(queries[half_rows:], "req", axis=0, tiled=True),
        lax.all_gather(fresh_kv[half_rows:], "req", axis=0, tiled=True),
    )
    flat_owners = far_owners.reshape(-1)
    picked = jnp.nonzero(flat_owners == device_index, size=half_rows)[0].astype(jnp.int32)
    request_ids = picked // half_rows * row_count + half_rows + picked % half_rows
    held_out = attend(
        jnp.take(sent_queries, picked, axis=0),
        jnp.take(sent_fresh, picked, axis=0),
        kv_cache,
        jnp.take(offsets, request_ids) - shard_start,
        jnp.take(lengths, request_ids),
    )
    returned = lax.all_gather(held_out, "req", axis=0, tiled=True)
    ordinal = device_index * half_rows + jnp.arange(half_rows, dtype=jnp.int32)
    earlier = jnp.arange(devices * half_rows, dtype=jnp.int32)[None, :] < ordinal[:, None]
    match_owner = flat_owners[None, :] == my_owners[:, None]
    rank_list = jnp.sum((earlier & match_owner).astype(jnp.int32), axis=1)
    remote_out = jnp.take(returned, my_owners * half_rows + rank_list, axis=0)
    attended = jnp.concatenate([local_out, remote_out], axis=0)
    partial_value = jnp.dot(attended, out_weight, preferred_element_type=jnp.float32)
    return lax.psum_scatter(
        partial_value.astype(jnp.bfloat16), "tp", scatter_dimension=1, tiled=True
    )


def solution(mesh):
    in_specs = (P("req", "tp"), P("req", "tp"), P("tp", None, "req"), P("tp", None), P(), P())
    out_specs = P("req", "tp")
    return jax.shard_map(shards, mesh=mesh, in_specs=in_specs, out_specs=out_specs, check_vma=False)
```

profile of v0, /device:TPU:2, one launch (start us, length us, event | category | flops | bytes accessed | tf_op | source)
XLA Modules:
  0.0 219.1 jit_solution(9321281883849411793)
XLA Ops:
  6.5 0.0 copy-start
  6.5 0.0 copy-start.1
  6.5 0.0 reduce-scatter.4.cloned.1.call-start
  6.5 0.8 add_select_fusion
  7.4 0.1 reshape.393
  7.4 0.7 fusion.70
  8.2 0.1 reshape.401
  8.3 0.3 reduce-window.12
  8.6 0.1 slice.49
  8.7 0.1 slice_reduce_fusion
  8.8 0.1 broadcast_add_fusion
  8.9 4.1 %scatter_custom_fusion = s32[8]{0:T(128)S(1)} fusion(s32[512]{0:T(512)S(1)} %bitcast.126, s32[512]{0:T(512)S(1)} %broadcast.332, s32[]{:T(128)} %constant.114.clone.1), kind=kCustom, calls=%fused_computation.118 | custom fusion | flops 512 | bytes 36 | tf_op jit(solution)/shard_map/scatter-add | solution.py:80
  13.0 0.2 select_n.123
  13.1 0.7 fusion.64
  13.8 0.7 compare_and_fusion.1
  14.5 0.7 fusion.72
  15.2 0.1 reshape.388
  15.3 0.7 fusion.71
  16.0 0.1 reshape.386
  16.1 0.1 fusion.55
  16.2 0.1 copy.31
  16.3 0.1 eq.29
  16.4 0.2 convert_reduce_fusion
  16.7 1.3 gather_fusion.1
  18.0 0.0 copy-done.1
  18.0 0.6 gather_fusion.2
  18.6 50.0 %all_gather.10 = bf16[512,160]{1,0:T(8,128)(2,1)S(1)} all-gather(bf16[8,160]{1,0:T(8,128)(2,1)S(1)} %get-tuple-element.23), channel_id=1, replica_groups=mesh['req'=64,'tp'=8] {'req'}, dimensions={0}, use_global_device_ids=true | all-gather | bytes 166400 | tf_op jit(solution)/shard_map/all_gather | solution.py:77
  68.6 0.6 gather_fusion
  69.2 0.1 gather.13
  69.3 0.1 copy_select_fusion
  69.4 45.3 %all_gather.9 = bf16[512,320]{1,0:T(8,128)(2,1)S(1)} all-gather(bf16[8,320]{1,0:T(8,128)(2,1)S(1)} %get-tuple-element.21), channel_id=1, replica_groups=mesh['req'=64,'tp'=8] {'req'}, dimensions={0}, use_global_device_ids=true | all-gather | bytes 332800 | tf_op jit(solution)/shard_map/all_gather | solution.py:76
  114.6 0.6 gather_fusion.3
  115.2 0.1 broadcast_select_fusion.1
  115.3 0.1 reshape.396
  115.4 0.1 fusion.56
  115.5 0.1 copy.33
  115.6 0.8 broadcast_add_fusion.1
  116.3 0.2 fusion.47
  116.5 0.0 copy-start.2
  116.5 2.0 fusion.73
  118.6 0.4 fusion.14
  118.9 0.0 copy-done.2
  119.0 0.6 fusion.37
  119.6 0.1 reshape.399
  119.7 48.0 %all_gather.11 = bf16[512,320]{1,0:T(8,128)(2,1)S(1)} all-gather(bf16[8,320]{1,0:T(8,128)(2,1)S(1)} %reshape.399), channel_id=1, replica_groups=mesh['req'=64,'tp'=8] {'req'}, dimensions={0}, use_global_device_ids=true | all-gather | bytes 332800 | tf_op jit(solution)/shard_map/all_gather | solution.py:89
  167.7 0.2 fusion.45
  167.9 0.0 copy-start.3
  167.9 2.0 fusion.74
  169.9 0.4 fusion.12
  170.3 0.0 copy-done.3
  170.3 0.6 fusion.34
  171.0 0.1 reshape.392
  171.1 0.6 gather_fusion.4
  171.7 0.1 broadcast_select_fusion
  171.7 0.0 copy-done
  171.7 0.3 convolution_convert_fusion
  172.1 1.1 copy.34
  173.2 0.0 reduce-scatter.4.cloned.1.call-update
  173.2 37.5 %reduce-scatter.4.cloned.1.call-done = bf16[320,16]{1,0:T(8,128)(2,1)} async-done(((bf16[2560,16]{1,0:T(8,128)(2,1)}), bf16[320,16]{1,0:T(8,128)(2,1)}) %reduce-scatter.4.cloned.1.call-update) | async-done | bytes 10256
  210.7 1.6 copy.35
  (19 shorter events, 0.2 us)
Async XLA Ops:
  6.5 165.2 %copy-start = (bf16[320,2560]{1,0:T(8,128)(2,1)S(1)}, bf16[320,2560]{1,0:T(8,128)(2,1)}, u32[]{:S(2)}) copy-start(bf16[320,2560]{1,0:T(8,128)(2,1)} %param.13) | copy-start | bytes 4915204
  6.5 11.5 %copy-start.1 = (s32[1024]{0:T(1024)S(1)}, s32[1024]{0:T(1024)}, u32[]{:S(2)}) copy-start(s32[1024]{0:T(1024)} %param.15) | copy-start | bytes 12292
  6.5 204.1 %reduce-scatter.4.cloned.1.call-start = ((), (), s32[]{:S(2)}) async-start(), calls=%async_computation.1 | async-start | bytes 737280
  116.5 2.5 %copy-start.2 = (bf16[1,160,10240]{2,1,0:T(8,128)(2,1)S(1)}, bf16[1,160,10240]{2,1,0:T(8,128)(2,1)}, u32[]{:S(2)}) copy-start(bf16[1,160,10240]{2,1,0:T(8,128)(2,1)} %param.12) | copy-start | bytes 9830404
  167.9 2.5 %copy-start.3 = (bf16[1,160,10240]{2,1,0:T(8,128)(2,1)S(1)}, bf16[1,160,10240]{2,1,0:T(8,128)(2,1)}, u32[]{:S(2)}) copy-start(bf16[1,160,10240]{2,1,0:T(8,128)(2,1)} %param.12) | copy-start | bytes 9830404
Sparse Core Ops, SparseCore 0:
  173.3 37.2 reduce-scatter.3
where the time goes:
time: 219 us
  blocking collectives  143 us (65%)
  waiting for transfers between devices  37.5 us (17%)
  between operations  13.5 us (6%)
  other arithmetic  9.94 us (5%)
  local copies, waits for them, and re-layouts  8.9 us (4%)
  matrix products  5.93 us (3%)
    all_gather x1, blocking collectives, shards(): lax.all_gather(fresh_kv[half_rows:], 'req', axis=0, tiled=True)  50 us
    all_gather x1, blocking collectives, shards(): returned = lax.all_gather(held_out, 'req', axis=0, tiled=True)  48 us
    all_gather x1, blocking collectives, shards(): lax.all_gather(queries[half_rows:], 'req', axis=0, tiled=True)  45.3 us
    unnamed x2, waiting for transfers between devices  37.5 us
  transfers between devices with their start and end apart: 1, of which 1 were waited for; matrix products, arithmetic and copies ran while one was open for 0% of the time, Pallas kernels for 0%

commit v1 on v0

--- a/solution.py
+++ b/solution.py
@@ -73,7 +73,10 @@
         lax.dynamic_slice_in_dim(lengths, home_first, half_rows),
     )
     sent_queries, sent_fresh = (
-        lax.all_gather(queries[half_rows:], "req", axis=0, tiled=True),
+        jnp.concatenate(
+            lax.all_to_all(jnp.stack([queries[half_rows:]] * lax.axis_size("req")), "req", 0, 0),
+            axis=0,
+        ),
         lax.all_gather(fresh_kv[half_rows:], "req", axis=0, tiled=True),
     )
     flat_owners = far_owners.reshape(-1)

time: 219 us -> 180 us (0.82)
  blocking collectives: 143 us -> 91.7 us
  starting transfers between devices: 0.01 us -> 13.9 us
    all_gather x1 -> x0, blocking collectives: 45.3 us -> none  [shards(): lax.all_gather(queries[half_rows:], 'req', axis=0, tiled=True)]
    all_to_all x0 -> x1, starting transfers between devices: none -> 13.9 us  [shards(): lax.all_to_all(jnp.stack([queries[half_rows:]] * lax.axis_size('req')), '...]
    all_gather x1, blocking collectives: 50 us -> 43.9 us  [shards(): lax.all_gather(fresh_kv[half_rows:], 'req', axis=0, tiled=True)]
  transfers between devices with their start and end apart: 1 -> 2, of which waited for: 1 -> 1; matrix products, arithmetic and copies ran while one was open for 0% -> 8% of each run, Pallas kernels for 0% -> 0%
where the time goes in v1:
time: 180 us
  blocking collectives  91.7 us (51%)
  waiting for transfers between devices  37.5 us (21%)
  starting transfers between devices  13.9 us (8%)
  between operations  13.6 us (8%)
  other arithmetic  9.13 us (5%)
  local copies, waits for them, and re-layouts  8.42 us (5%)
  matrix products  5.93 us (3%)
    all_gather x1, blocking collectives, shards(): returned = lax.all_gather(held_out, 'req', axis=0, tiled=True)  47.8 us
    all_gather x1, blocking collectives, shards(): lax.all_gather(fresh_kv[half_rows:], 'req', axis=0, tiled=True)  43.9 us
    unnamed x2, waiting for transfers between devices  37.5 us
    all_to_all x1, starting transfers between devices, shards(): lax.all_to_all(jnp.stack([queries[half_rows:]] * lax.axis_size('req')), '...  13.9 us
    scatter-add x1, other arithmetic, shards(): jnp.nonzero(flat_owners == device_index, size=half_rows)[0]  4.09 us
    dot_general x2, matrix products, attend(): jnp.einsum('nhgd,hdt->hngt', grouped, cache_block[:, :HD, :], preferred_e...  4.07 us
  transfers between devices with their start and end apart: 2, of which 1 were waited for; matrix products, arithmetic and copies ran while one was open for 8% of the time, Pallas kernels for 0%

profile of v1, /device:TPU:2, one launch (start us, length us, event | category | flops | bytes accessed | tf_op | source)
XLA Modules:
  0.0 180.1 jit_solution(3478192577665686892)
XLA Ops:
  6.5 0.0 copy-start
  6.5 0.0 copy-start.1
  6.5 0.0 copy-start.5
  6.5 0.0 copy-start.2
  6.5 0.9 fusion.71
  7.4 0.8 stack.2
  8.2 13.9 %all-to-all-start = ((bf16[64,8,320]{2,1,0:T(8,128)(2,1)}), bf16[64,8,320]{2,1,0:T(8,128)(2,1)S(1)}, u32[]{:S(2)}, u32[]{:S(2)}) async-start(bf16[64,8,320]{2,1,0:T(8,128)(2,1)} %stack.2), calls=%async_computation | async-start | bytes 786432 | tf_op jit(solution)/shard_map/all_to_all | solution.py:77
  22.0 0.0 reduce-scatter.4.cloned.1.call-start
  22.1 0.7 add_select_fusion
  22.8 0.1 reshape.398
  22.9 0.7 fusion.70
  23.6 0.1 reshape.407
  23.7 0.3 reduce-window.12
  24.0 0.1 slice.49
  24.1 0.1 slice_reduce_fusion
  24.2 0.1 broadcast_add_fusion
  24.3 4.1 %scatter_custom_fusion = s32[8]{0:T(128)S(1)} fusion(s32[512]{0:T(512)S(1)} %bitcast.128, s32[512]{0:T(512)S(1)} %broadcast.334, s32[]{:T(128)} %constant.114.clone.1), kind=kCustom, calls=%fused_computation.118 | custom fusion | flops 512 | bytes 36 | tf_op jit(solution)/shard_map/scatter-add | solution.py:83
  28.4 0.2 select_n.123
  28.6 0.7 fusion.64
  29.2 0.7 compare_and_fusion.1
  29.9 0.0 copy-done.5
  29.9 0.1 reshape.393
  30.0 0.1 reshape.391
  30.1 0.1 fusion.55
  30.2 0.1 copy.31
  30.3 0.1 eq.29
  30.4 0.2 convert_reduce_fusion
  30.7 0.0 copy-done.1
  30.7 0.6 gather_fusion.1
  31.3 0.0 copy-done.2
  31.3 0.6 gather_fusion.2
  32.0 43.9 %all_gather.6 = bf16[512,160]{1,0:T(8,128)(2,1)S(1)} all-gather(bf16[8,160]{1,0:T(8,128)(2,1)S(1)} %get-tuple-element.23), channel_id=1, replica_groups=mesh['req'=64,'tp'=8] {'req'}, dimensions={0}, use_global_device_ids=true | all-gather | bytes 166400 | tf_op jit(solution)/shard_map/all_gather | solution.py:80
  75.8 0.6 gather_fusion
  76.4 0.1 gather.13
  76.5 0.1 broadcast_add_fusion.1
  76.5 0.2 fusion.45
  76.7 0.0 copy-start.3
  76.7 2.0 %fusion.74 = (f32[8,4]{0,1:T(4,128)S(1)}, f32[8,4,10240]{2,0,1:T(8,128)S(1)}) fusion(bf16[1,160,10240]{2,1,0:T(8,128)(2,1)} %param.12, bf16[8,4,80]{2,1,0:T(4,128)(2,1)S(1)} %reshape.391, pred[8,10240]{1,0:T(8,128)(4,1)S(1)} %fusion.45), kind=kOutput, calls=%fused_computation.127 | convolution fusion | flops 53411808 | bytes 3036288 | tf_op jit(solution)/shard_map/nhgd,hdt->hngt/dot_general | solution.py:18
  78.8 0.4 fusion.12
  79.2 0.0 copy-done.3
  79.2 0.6 fusion.34
  79.8 0.1 reshape.397
  79.9 0.2 fusion.47
  80.1 0.1 copy_select_fusion
  80.2 0.0 all-to-all-done
  80.2 0.6 gather_fusion.3
  80.8 0.1 broadcast_select_fusion.1
  80.9 0.1 reshape.402
  80.9 0.1 fusion.56
  81.1 0.1 copy.33
  81.1 2.0 %fusion.73 = (f32[8,4]{0,1:T(4,128)S(1)}, f32[8,4,10240]{2,0,1:T(8,128)S(1)}) fusion(bf16[1,160,10240]{2,1,0:T(8,128)(2,1)} %param.12, bf16[8,4,80]{2,1,0:T(4,128)(2,1)S(1)} %reshape.402, pred[8,10240]{1,0:T(8,128)(4,1)S(1)} %fusion.47), kind=kOutput, calls=%fused_computation.126 | convolution fusion | flops 53411808 | bytes 3036288 | tf_op jit(solution)/shard_map/nhgd,hdt->hngt/dot_general | solution.py:18
  83.2 0.4 fusion.14
  83.6 0.0 copy-done.4
  83.6 0.6 fusion.37
  84.2 0.1 reshape.405
  84.3 47.8 %all_gather.7 = bf16[512,320]{1,0:T(8,128)(2,1)S(1)} all-gather(bf16[8,320]{1,0:T(8,128)(2,1)S(1)} %reshape.405), channel_id=1, replica_groups=mesh['req'=64,'tp'=8] {'req'}, dimensions={0}, use_global_device_ids=true | all-gather | bytes 332800 | tf_op jit(solution)/shard_map/all_gather | solution.py:92
  132.2 0.6 gather_fusion.4
  132.7 0.1 broadcast_select_fusion
  132.8 0.0 copy-done
  132.8 0.3 convolution_convert_fusion
  133.2 1.1 copy.34
  134.3 0.0 reduce-scatter.4.cloned.1.call-update
  134.3 37.5 %reduce-scatter.4.cloned.1.call-done = bf16[320,16]{1,0:T(8,128)(2,1)} async-done(((bf16[2560,16]{1,0:T(8,128)(2,1)}), bf16[320,16]{1,0:T(8,128)(2,1)}) %reduce-scatter.4.cloned.1.call-update) | async-done | bytes 10256
  171.7 1.6 copy.35
  (21 shorter events, 0.2 us)
Async XLA Ops:
  6.5 126.3 %copy-start = (bf16[320,2560]{1,0:T(8,128)(2,1)S(1)}, bf16[320,2560]{1,0:T(8,128)(2,1)}, u32[]{:S(2)}) copy-start(bf16[320,2560]{1,0:T(8,128)(2,1)} %param.13) | copy-start | bytes 4915204
  6.5 24.1 %copy-start.1 = (s32[1024]{0:T(1024)S(1)}, s32[1024]{0:T(1024)}, u32[]{:S(2)}) copy-start(s32[1024]{0:T(1024)} %param.14) | copy-start | bytes 12292
  6.5 23.4 %copy-start.5 = (bf16[16,160]{1,0:T(8,128)(2,1)S(1)}, bf16[16,160]{1,0:T(8,128)(2,1)}, u32[]{:S(2)}) copy-start(bf16[16,160]{1,0:T(8,128)(2,1)} %param.11) | copy-start | bytes 15364
  6.5 24.8 %copy-start.2 = (s32[1024]{0:T(1024)S(1)}, s32[1024]{0:T(1024)}, u32[]{:S(2)}) copy-start(s32[1024]{0:T(1024)} %param.15) | copy-start | bytes 12292
  8.2 72.0 %all-to-all-start = ((bf16[64,8,320]{2,1,0:T(8,128)(2,1)}), bf16[64,8,320]{2,1,0:T(8,128)(2,1)S(1)}, u32[]{:S(2)}, u32[]{:S(2)}) async-start(bf16[64,8,320]{2,1,0:T(8,128)(2,1)} %stack.2), calls=%async_computation | async-start | bytes 786432 | tf_op jit(solution)/shard_map/all_to_all | solution.py:77
  22.0 149.7 %reduce-scatter.4.cloned.1.call-start = ((), (), s32[]{:S(2)}) async-start(), calls=%async_computation.2 | async-start | bytes 737280
  76.7 2.5 %copy-start.3 = (bf16[1,160,10240]{2,1,0:T(8,128)(2,1)S(1)}, bf16[1,160,10240]{2,1,0:T(8,128)(2,1)}, u32[]{:S(2)}) copy-start(bf16[1,160,10240]{2,1,0:T(8,128)(2,1)} %param.12) | copy-start | bytes 9830404
  81.1 2.4 %copy-start.4 = (bf16[1,160,10240]{2,1,0:T(8,128)(2,1)S(1)}, bf16[1,160,10240]{2,1,0:T(8,128)(2,1)}, u32[]{:S(2)}) copy-start(bf16[1,160,10240]{2,1,0:T(8,128)(2,1)} %param.12) | copy-start | bytes 9830404
Sparse Core Ops, SparseCore 0:
  134.4 37.2 reduce-scatter.3
